TPU v7x, 512 devices: a whole 4x8x8 slice. The times are simulated.
512 devices in a mesh: term: 8 (over z), sector: 64 (over x, y, core).
Axes of the slice: x: 4, y: 8, z: 8, core: 2. Of those that a mesh axis runs over, the one named last changes fastest.
Arguments:
- wave_tiles: bfloat16 [1024, 2, 128, 128], P('sector'), may hold values from -6 to 6
- left_env: bfloat16 [8, 64, 128, 128], P('term', 'sector'), may hold values from -0.5 to 0.5
- right_env: bfloat16 [8, 64, 128, 128], P('term', 'sector'), may hold values from -0.5 to 0.5
- send_list: int32 [64, 128], P('sector'), may hold values from -1 to 15, as said below
- left_tasks: int32 [8, 64, 96, 3], P('term', 'sector'), may hold values from 0 to 127, as said below
- right_tasks: int32 [8, 64, 256, 3], P('term', 'sector'), may hold values from 0 to 63, as said below
Outputs:
- sigma: float32 [1024, 2, 128, 128], P('sector', None, 'term')
Inputs may be any that keep to these rules, and one draw needn't show every extreme that they name: send_list[s, o * 2 + c] is a tile index local to sender s, or -1 for an empty slot; some owner drawn from the seed receives a full 2 tiles from every sender. `left_tasks`: entries 0, 1, 2 lie below 64, 128 and 32. `right_tasks`: entries 0, 1, 2 lie below 32, 64 and 16.
All inputs are finite; a program needn't handle non-finite values.
Results may differ from a plain program's by a relative error of at most 0.0029.
Values may be sent and summed in bfloat16 or wider, within the bound.
A program may use at most 128 MiB of HBM per device.

v0:
```python
import math
import jax
import jax.numpy as jnp
from jax import lax
from jax.sharding import PartitionSpec as P

INTER_TILES = 32


def run_tasks(tasks, first_tiles, second_tiles, contract, count):
    block = math.gcd(tasks.shape[0], 32)
    shape = (count,) + tuple(contract(first_tiles[:1], second_tiles[:1]).shape[1:])

    def step(turn, total):
        rows = lax.dynamic_slice_in_dim(tasks, turn * block, block, 0)
        first = jnp.take(first_tiles, rows[:, 0], axis=0)
        second = jnp.take(second_tiles, rows[:, 1], axis=0)
        return total.at[rows[:, 2]].add(contract(first, second))

    return lax.fori_loop(0, tasks.shape[0] // block, step, jnp.zeros(shape, jnp.float32))


def left_product(env_part, wave_part):
    return jnp.einsum("bij,bvjk->bvik", env_part, wave_part, preferred_element_type=jnp.float32)


def right_product(inter_part, env_part):
    return jnp.einsum("bvij,bjk->bvik", inter_part, env_part, preferred_element_type=jnp.float32)


def shards(wave_tiles, left_env, right_env, send_list, left_tasks, right_tasks):
    env_left, env_right = (
        lax.all_gather(left_env, "sector", axis=1, tiled=True),
        lax.all_gather(right_env, "sector", axis=1, tiled=True),
    )
    env_left = env_left[0]
    env_right = env_right[0]
    slot_list = send_list[0]
    live = slot_list >= 0
    picked = jnp.take(wave_tiles, jnp.maximum(slot_list, 0), axis=0)
    outgoing = jnp.where(live[:, None, None, None], picked, jnp.zeros((), jnp.bfloat16))
    tile_dim = wave_tiles.shape[2]
    groups = lax.axis_size("term")
    share = tile_dim // groups
    received = lax.all_to_all(outgoing, "sector", split_axis=0, concat_axis=0, tiled=True)
    inter = run_tasks(left_tasks[0, 0], env_left, received, left_product, INTER_TILES).astype(
        jnp.bfloat16
    )
    partial_value = run_tasks(
        right_tasks[0, 0], inter, env_right, right_product, wave_tiles.shape[0]
    )
    summed = lax.psum(partial_value, "term")
    return lax.dynamic_slice_in_dim(summed, lax.axis_index("term") * share, share, 2)


def solution(mesh):
    in_specs = (
        P("sector", None, None, None),
        P("term", "sector", None, None),
        P("term", "sector", None, None),
        P("sector", None),
        P("term", "sector", None, None),
        P("term", "sector", None, None),
    )
    out_specs = P("sector", None, "term", None)
    return jax.shard_map(shards, mesh=mesh, in_specs=in_specs, out_specs=out_specs, check_vma=False)
```

profile of v0, /device:TPU:2, one launch (start us, length us, event | category | flops | bytes accessed | tf_op | source)
XLA Modules:
  0.0 562.8 jit_solution(14975568767976974510)
XLA Ops:
  8.0 6.5 %gather_fusion.4 = bf16[128,2,128,128]{3,2,1,0:T(8,128)(2,1)} fusion(bf16[16,2,128,128]{3,2,1,0:T(8,128)(2,1)S(1)} %copy-done, s32[1024]{0:T(1024)S(1)} %pad_clamp_fusion.4), kind=kCustom, calls=%fused_computation.4 | custom fusion | bytes 16777728 | tf_op jit(solution)/shard_map/jit(_take)/gather | solution.py:40
  14.5 7.5 %select_select_fusion = bf16[128,2,128,128]{3,2,1,0:T(8,128)(2,1)} fusion(bf16[128,2,128,128]{3,2,1,0:T(8,128)(2,1)} %gather_fusion.4, pred[128]{0:T(512)(128)(4,1)S(1)} %get-tuple-element.225, pred[128]{0:T(512)(128)(4,1)S(1)} %get-tuple-element.224), kind=kLoop, calls=%fused_computation.45 | loop fusion | flops 8388608 | bytes 16777472 | tf_op jit(solution)/shard_map/jit(_where)/select_n | solution.py:41
  22.0 11.3 %all-to-all-start = ((bf16[128,2,128,128]{3,2,1,0:T(8,128)(2,1)}), bf16[128,2,128,128]{3,2,1,0:T(8,128)(2,1)}, u32[]{:S(2)}, u32[]{:S(2)}) async-start(bf16[128,2,128,128]{3,2,1,0:T(8,128)(2,1)} %select_select_fusion), calls=%async_computation | async-start | bytes 16777216 | tf_op jit(solution)/shard_map/all_to_all | solution.py:45
  34.8 102.3 %all-gather.3.cloned.1.call-done = bf16[1,64,128,128]{3,2,0,1:T(8,128)(2,1)} async-done(((bf16[1,1,128,128]{3,2,0,1:T(8,128)(2,1)}), bf16[1,64,128,128]{3,2,0,1:T(8,128)(2,1)}) %all-gather.3.cloned.1.call-update) | async-done | bytes 2097168 | tf_op jit(solution)/shard_map/all_gather | solution.py:33
  137.1 90.6 %all-to-all-done = bf16[128,2,128,128]{3,2,1,0:T(8,128)(2,1)} async-done(((bf16[128,2,128,128]{3,2,1,0:T(8,128)(2,1)}), bf16[128,2,128,128]{3,2,1,0:T(8,128)(2,1)}, u32[]{:S(2)}, u32[]{:S(2)}) %all-to-all-start) | async-done | bytes 8388640 | tf_op jit(solution)/shard_map/all_to_all | solution.py:45
  230.2 82.3 %while.26 = (s32[]{:T(128)}, f32[32,2,128,128]{3,2,1,0:T(8,128)}, s32[96,3]{0,1:T(4,128)S(1)}, bf16[128,2,128,128]{3,2,1,0:T(8,128)(2,1)}, bf16[64,128,128]{2,1,...) while((s32[]{:T(128)}, f32[32,2,128,128]{3,2,1,0:T(8,128)}, s32[96,3]{0,1:T(4,128)S(1)}, ...), condition=%wide.region_2.4_spmd, body=%wide.region_0.3_spmd.sunk | while | flops 271059520 | bytes 34613776 | solution.py:20
  230.3 4.4 gather_fusion
  242.1 5.6 copy.23
  247.7 10.1 %scatter_fusion = f32[32,2,128,128]{3,2,1,0:T(8,128)} fusion(f32[32,2,128,128]{3,2,1,0:T(8,128)} %get-tuple-element.314, s32[32]{0:T(128)S(1)} %get-tuple-element.291, f32[32,2,128,128]{3,2,1,0:T(8,128)} %copy.23), kind=kCustom, calls=%fused_computation.5.clone.1 | custom fusion | flops 1048576 | bytes 12583040 | tf_op jit(solution)/shard_map/while/body/eval_jaxpr/scatter-add | solution.py:18
  257.9 4.3 gather_fusion
  269.6 5.6 copy.23
  275.2 9.9 %scatter_fusion = f32[32,2,128,128]{3,2,1,0:T(8,128)} fusion(f32[32,2,128,128]{3,2,1,0:T(8,128)} %get-tuple-element.314, s32[32]{0:T(128)S(1)} %get-tuple-element.291, f32[32,2,128,128]{3,2,1,0:T(8,128)} %copy.23), kind=kCustom, calls=%fused_computation.5.clone.1 | custom fusion | flops 1048576 | bytes 12583040 | tf_op jit(solution)/shard_map/while/body/eval_jaxpr/scatter-add | solution.py:18
  296.9 5.6 copy.23
  302.6 9.9 %scatter_fusion = f32[32,2,128,128]{3,2,1,0:T(8,128)} fusion(f32[32,2,128,128]{3,2,1,0:T(8,128)} %get-tuple-element.314, s32[32]{0:T(128)S(1)} %get-tuple-element.291, f32[32,2,128,128]{3,2,1,0:T(8,128)} %copy.23), kind=kCustom, calls=%fused_computation.5.clone.1 | custom fusion | flops 1048576 | bytes 12583040 | tf_op jit(solution)/shard_map/while/body/eval_jaxpr/scatter-add | solution.py:18
  316.6 145.3 %while.27 = (s32[]{:T(128)}, f32[16,2,128,128]{3,2,1,0:T(8,128)S(1)}, s32[256,3]{0,1:T(4,128)S(1)}, bf16[32,2,128,128]{3,2,1,0:T(8,128)(2,1)}, bf16[64,128,128]{...) while((s32[]{:T(128)}, f32[16,2,128,128]{3,2,1,0:T(8,128)S(1)}, ...), condition=%wide.region_5.7_spmd, body=%wide.region_3.6_spmd.sunk | while | flops 271059520 | bytes 26225168 | solution.py:20
  323.7 4.6 fusion.34
  328.3 6.5 %scatter_fusion.1 = f32[16,2,128,128]{3,2,1,0:T(8,128)S(1)} fusion(f32[16,2,128,128]{3,2,1,0:T(8,128)S(1)} %get-tuple-element.341, s32[32]{0:T(128)S(1)} %get-tuple-element.300, f32[32,2,128,128]{3,2,1,0:T(8,128)} %fusion.34), kind=kCustom, calls=%fused_computation.6.clone.1 | custom fusion | flops 1048576 | bytes 12583040 | tf_op jit(solution)/shard_map/while/body/eval_jaxpr/scatter-add | solution.py:18
  341.9 4.6 fusion.34
  346.5 6.5 %scatter_fusion.1 = f32[16,2,128,128]{3,2,1,0:T(8,128)S(1)} fusion(f32[16,2,128,128]{3,2,1,0:T(8,128)S(1)} %get-tuple-element.341, s32[32]{0:T(128)S(1)} %get-tuple-element.300, f32[32,2,128,128]{3,2,1,0:T(8,128)} %fusion.34), kind=kCustom, calls=%fused_computation.6.clone.1 | custom fusion | flops 1048576 | bytes 12583040 | tf_op jit(solution)/shard_map/while/body/eval_jaxpr/scatter-add | solution.py:18
  360.0 4.6 fusion.34
  364.6 6.5 %scatter_fusion.1 = f32[16,2,128,128]{3,2,1,0:T(8,128)S(1)} fusion(f32[16,2,128,128]{3,2,1,0:T(8,128)S(1)} %get-tuple-element.341, s32[32]{0:T(128)S(1)} %get-tuple-element.300, f32[32,2,128,128]{3,2,1,0:T(8,128)} %fusion.34), kind=kCustom, calls=%fused_computation.6.clone.1 | custom fusion | flops 1048576 | bytes 12583040 | tf_op jit(solution)/shard_map/while/body/eval_jaxpr/scatter-add | solution.py:18
  378.2 4.6 fusion.34
  382.8 6.5 %scatter_fusion.1 = f32[16,2,128,128]{3,2,1,0:T(8,128)S(1)} fusion(f32[16,2,128,128]{3,2,1,0:T(8,128)S(1)} %get-tuple-element.341, s32[32]{0:T(128)S(1)} %get-tuple-element.300, f32[32,2,128,128]{3,2,1,0:T(8,128)} %fusion.34), kind=kCustom, calls=%fused_computation.6.clone.1 | custom fusion | flops 1048576 | bytes 12583040 | tf_op jit(solution)/shard_map/while/body/eval_jaxpr/scatter-add | solution.py:18
  396.4 4.6 fusion.34
  400.9 6.5 %scatter_fusion.1 = f32[16,2,128,128]{3,2,1,0:T(8,128)S(1)} fusion(f32[16,2,128,128]{3,2,1,0:T(8,128)S(1)} %get-tuple-element.341, s32[32]{0:T(128)S(1)} %get-tuple-element.300, f32[32,2,128,128]{3,2,1,0:T(8,128)} %fusion.34), kind=kCustom, calls=%fused_computation.6.clone.1 | custom fusion | flops 1048576 | bytes 12583040 | tf_op jit(solution)/shard_map/while/body/eval_jaxpr/scatter-add | solution.py:18
  414.5 4.6 fusion.34
  419.1 6.5 %scatter_fusion.1 = f32[16,2,128,128]{3,2,1,0:T(8,128)S(1)} fusion(f32[16,2,128,128]{3,2,1,0:T(8,128)S(1)} %get-tuple-element.341, s32[32]{0:T(128)S(1)} %get-tuple-element.300, f32[32,2,128,128]{3,2,1,0:T(8,128)} %fusion.34), kind=kCustom, calls=%fused_computation.6.clone.1 | custom fusion | flops 1048576 | bytes 12583040 | tf_op jit(solution)/shard_map/while/body/eval_jaxpr/scatter-add | solution.py:18
  432.7 4.6 fusion.34
  437.2 6.5 %scatter_fusion.1 = f32[16,2,128,128]{3,2,1,0:T(8,128)S(1)} fusion(f32[16,2,128,128]{3,2,1,0:T(8,128)S(1)} %get-tuple-element.341, s32[32]{0:T(128)S(1)} %get-tuple-element.300, f32[32,2,128,128]{3,2,1,0:T(8,128)} %fusion.34), kind=kCustom, calls=%fused_computation.6.clone.1 | custom fusion | flops 1048576 | bytes 12583040 | tf_op jit(solution)/shard_map/while/body/eval_jaxpr/scatter-add | solution.py:18
  450.8 4.6 fusion.34
  455.4 6.5 %scatter_fusion.1 = f32[16,2,128,128]{3,2,1,0:T(8,128)S(1)} fusion(f32[16,2,128,128]{3,2,1,0:T(8,128)S(1)} %get-tuple-element.341, s32[32]{0:T(128)S(1)} %get-tuple-element.300, f32[32,2,128,128]{3,2,1,0:T(8,128)} %fusion.34), kind=kCustom, calls=%fused_computation.6.clone.1 | custom fusion | flops 1048576 | bytes 12583040 | tf_op jit(solution)/shard_map/while/body/eval_jaxpr/scatter-add | solution.py:18
  463.2 91.4 %all-reduce.2.cloned.1.call-done = f32[16,2,128,128]{3,2,1,0:T(8,128)} async-done(((f32[16,2,128,128]{3,2,1,0:T(8,128)}), f32[16,2,128,128]{3,2,1,0:T(8,128)}) %all-reduce.2.cloned.1.call-update) | async-done | bytes 2097168 | tf_op jit(solution)/shard_map/psum | solution.py:52
  (113 shorter events, 95.7 us)
Async XLA Ops:
  6.5 1.4 copy-start
  22.0 12.8 %copy-start.3 = (s32[1,1,96,3]{2,1,3,0:T(1,128)S(1)}, s32[1,1,96,3]{2,1,3,0:T(1,128)}, u32[]{:S(2)}) copy-start(s32[1,1,96,3]{2,1,3,0:T(1,128)} %param.16) | copy-start | bytes 3460
  22.0 12.8 %copy-start.2 = (s32[1,1,256,3]{2,1,3,0:T(1,128)S(1)}, s32[1,1,256,3]{2,1,3,0:T(1,128)}, u32[]{:S(2)}) copy-start(s32[1,1,256,3]{2,1,3,0:T(1,128)} %param.17) | copy-start | bytes 9220
  22.0 205.8 %all-to-all-start = ((bf16[128,2,128,128]{3,2,1,0:T(8,128)(2,1)}), bf16[128,2,128,128]{3,2,1,0:T(8,128)(2,1)}, u32[]{:S(2)}, u32[]{:S(2)}) async-start(bf16[128,2,128,128]{3,2,1,0:T(8,128)(2,1)} %select_select_fusion), calls=%async_computation | async-start | bytes 16777216 | tf_op jit(solution)/shard_map/all_to_all | solution.py:45
  33.3 103.9 %all-gather.3.cloned.1.call-start = ((), (), s32[]{:S(2)}) async-start(), calls=%async_computation.1 | async-start | bytes 2129920 | tf_op jit(solution)/shard_map/all_gather | solution.py:33
  34.0 282.4 %all-gather.5.cloned.1.call-start = ((), (), s32[]{:S(2)}) async-start(), calls=%async_computation.2 | async-start | bytes 2129920 | tf_op jit(solution)/shard_map/all_gather | solution.py:34
  34.8 519.8 %all-reduce.2.cloned.1.call-start = ((), (), s32[]{:S(2)}) async-start(), calls=%async_computation.3 | async-start | bytes 4194304 | tf_op jit(solution)/shard_map/psum | solution.py:52
  461.9 1.3 copy-start.1
Sparse Core Ops, SparseCore 0:
  37.5 99.6 all-gather.2
  140.5 95.8 all-gather.4
  463.3 91.2 all-reduce.1
where the time goes:
time: 565 us; the launch traced here: 563 us
  waiting for transfers between devices  286 us (51%)
  local copies, waits for them, and re-layouts  109 us (19%)
  other arithmetic  95 us (17%)
  matrix products  48.7 us (9%)
  between operations  13.2 us (2%)
  starting transfers between devices  11.4 us (2%)
    all_gather x1, waiting for transfers between devices, shards(): lax.all_gather(left_env, 'sector', axis=1, tiled=True)  102 us
    psum x1, waiting for transfers between devices, shards(): summed = lax.psum(partial_value, 'term')  91.4 us
    all_to_all x1, waiting for transfers between devices, shards(): lax.all_to_all(outgoing, 'sector', split_axis=0, concat_axis=0, tiled=True)  90.6 us
    scatter-add x11, other arithmetic, step(): return total.at[rows[:, 2]].add(contract(first, second))  81.8 us
    gather x11, local copies, waits for them, and re-layouts, step(): first = jnp.take(first_tiles, rows[:, 0], axis=0)  39.8 us
    gather x11, local copies, waits for them, and re-layouts, step(): second = jnp.take(second_tiles, rows[:, 1], axis=0)  38.9 us
    dot_general x8, matrix products, right_product(): jnp.einsum('bvij,bjk->bvik', inter_part, env_part, preferred_element_type...  36.6 us
    transpose x3, local copies, waits for them, and re-layouts, left_product(): jnp.einsum('bij,bvjk->bvik', env_part, wave_part, preferred_element_type=...  16.9 us
  transfers between devices with their start and end apart: 4, of which 3 were waited for; matrix products, arithmetic and copies ran while one was open for 16% of the time, Pallas kernels for 0%

commit v1 on v0

--- a/solution.py
+++ b/solution.py
@@ -49,7 +49,8 @@
     partial_value = run_tasks(
         right_tasks[0, 0], inter, env_right, right_product, wave_tiles.shape[0]
     )
-    summed = lax.psum(partial_value, "term")
+    parts = lax.all_gather(partial_value, "term")
+    summed = jnp.sum(parts, axis=0)
     return lax.dynamic_slice_in_dim(summed, lax.axis_index("term") * share, share, 2)
 
 

time: 565 us -> 645 us (1.14)
  the two profiles are of different devices: /device:TPU:2 before, /device:TPU:1 now
where the time goes in v1:
time: 645 us; the launch traced here: 643 us
  waiting for transfers between devices  373 us (58%)
  other arithmetic  103 us (16%)
  local copies, waits for them, and re-layouts  97.5 us (15%)
  matrix products  43 us (7%)
  between operations  13.2 us (2%)
  starting transfers between devices  12.4 us (2%)
    all_gather x1, waiting for transfers between devices, shards(): parts = lax.all_gather(partial_value, 'term')  177 us
    all_gather x1, waiting for transfers between devices, shards(): lax.all_gather(left_env, 'sector', axis=1, tiled=True)  109 us
    all_to_all x1, waiting for transfers between devices, shards(): lax.all_to_all(outgoing, 'sector', split_axis=0, concat_axis=0, tiled=True)  85.9 us
    scatter-add x11, other arithmetic, step(): return total.at[rows[:, 2]].add(contract(first, second))  81.9 us
    gather x11, local copies, waits for them, and re-layouts, step(): first = jnp.take(first_tiles, rows[:, 0], axis=0)  36.8 us
    dot_general x8, matrix products, right_product(): jnp.einsum('bvij,bjk->bvik', inter_part, env_part, preferred_element_type...  34.6 us
    gather x11, local copies, waits for them, and re-layouts, step(): second = jnp.take(second_tiles, rows[:, 1], axis=0)  31.7 us
    transpose x3, local copies, waits for them, and re-layouts, left_product(): jnp.einsum('bij,bvjk->bvik', env_part, wave_part, preferred_element_type=...  16.8 us
  transfers between devices with their start and end apart: 4, of which 3 were waited for; matrix products, arithmetic and copies ran while one was open for 13% of the time, Pallas kernels for 0%

profile of v1, /device:TPU:1, one launch (start us, length us, event | category | flops | bytes accessed | tf_op | source)
XLA Modules:
  0.0 643.0 jit_solution(10165461063882548504)
XLA Ops:
  8.0 6.5 %gather_fusion.4 = bf16[128,2,128,128]{3,2,1,0:T(8,128)(2,1)} fusion(bf16[16,2,128,128]{3,2,1,0:T(8,128)(2,1)S(1)} %copy-done, s32[1024]{0:T(1024)S(1)} %pad_clamp_fusion.4), kind=kCustom, calls=%fused_computation.4 | custom fusion | bytes 16777728 | tf_op jit(solution)/shard_map/jit(_take)/gather | solution.py:40
  14.5 7.5 %select_select_fusion = bf16[128,2,128,128]{3,2,1,0:T(8,128)(2,1)} fusion(bf16[128,2,128,128]{3,2,1,0:T(8,128)(2,1)} %gather_fusion.4, pred[128]{0:T(512)(128)(4,1)S(1)} %get-tuple-element.225, pred[128]{0:T(512)(128)(4,1)S(1)} %get-tuple-element.224), kind=kLoop, calls=%fused_computation.45 | loop fusion | flops 8388608 | bytes 16777472 | tf_op jit(solution)/shard_map/jit(_where)/select_n | solution.py:41
  22.0 12.1 %all-to-all-start = ((bf16[128,2,128,128]{3,2,1,0:T(8,128)(2,1)}), bf16[128,2,128,128]{3,2,1,0:T(8,128)(2,1)}, u32[]{:S(2)}, u32[]{:S(2)}) async-start(bf16[128,2,128,128]{3,2,1,0:T(8,128)(2,1)} %select_select_fusion), calls=%async_computation | async-start | bytes 16777216 | tf_op jit(solution)/shard_map/all_to_all | solution.py:45
  35.9 109.1 %all-gather.5.cloned.1.call-done = bf16[1,64,128,128]{3,2,0,1:T(8,128)(2,1)} async-done(((bf16[1,1,128,128]{3,2,0,1:T(8,128)(2,1)}), bf16[1,64,128,128]{3,2,0,1:T(8,128)(2,1)}) %all-gather.5.cloned.1.call-update) | async-done | bytes 2097168 | tf_op jit(solution)/shard_map/all_gather | solution.py:33
  145.0 85.9 %all-to-all-done = bf16[128,2,128,128]{3,2,1,0:T(8,128)(2,1)} async-done(((bf16[128,2,128,128]{3,2,1,0:T(8,128)(2,1)}), bf16[128,2,128,128]{3,2,1,0:T(8,128)(2,1)}, u32[]{:S(2)}, u32[]{:S(2)}) %all-to-all-start) | async-done | bytes 8388640 | tf_op jit(solution)/shard_map/all_to_all | solution.py:45
  233.4 75.7 %while.26 = (s32[]{:T(128)}, f32[32,2,128,128]{3,2,1,0:T(8,128)}, s32[96,3]{0,1:T(4,128)S(1)}, bf16[128,2,128,128]{3,2,1,0:T(8,128)(2,1)}, bf16[64,128,128]{2,1,...) while((s32[]{:T(128)}, f32[32,2,128,128]{3,2,1,0:T(8,128)}, s32[96,3]{0,1:T(4,128)S(1)}, ...), condition=%wide.region_2.4_spmd, body=%wide.region_0.3_spmd.sunk | while | flops 271059520 | bytes 34613776 | solution.py:20
  233.5 4.3 gather_fusion
  243.0 5.6 copy.23
  248.7 10.0 %scatter_fusion = f32[32,2,128,128]{3,2,1,0:T(8,128)} fusion(f32[32,2,128,128]{3,2,1,0:T(8,128)} %get-tuple-element.314, s32[32]{0:T(128)S(1)} %get-tuple-element.291, f32[32,2,128,128]{3,2,1,0:T(8,128)} %copy.23), kind=kCustom, calls=%fused_computation.5.clone.1 | custom fusion | flops 1048576 | bytes 12583040 | tf_op jit(solution)/shard_map/while/body/eval_jaxpr/scatter-add | solution.py:18
  258.7 4.3 gather_fusion
  268.2 5.6 copy.23
  273.9 10.1 %scatter_fusion = f32[32,2,128,128]{3,2,1,0:T(8,128)} fusion(f32[32,2,128,128]{3,2,1,0:T(8,128)} %get-tuple-element.314, s32[32]{0:T(128)S(1)} %get-tuple-element.291, f32[32,2,128,128]{3,2,1,0:T(8,128)} %copy.23), kind=kCustom, calls=%fused_computation.5.clone.1 | custom fusion | flops 1048576 | bytes 12583040 | tf_op jit(solution)/shard_map/while/body/eval_jaxpr/scatter-add | solution.py:18
  284.0 4.3 gather_fusion
  293.5 5.6 copy.23
  299.1 10.0 %scatter_fusion = f32[32,2,128,128]{3,2,1,0:T(8,128)} fusion(f32[32,2,128,128]{3,2,1,0:T(8,128)} %get-tuple-element.314, s32[32]{0:T(128)S(1)} %get-tuple-element.291, f32[32,2,128,128]{3,2,1,0:T(8,128)} %copy.23), kind=kCustom, calls=%fused_computation.5.clone.1 | custom fusion | flops 1048576 | bytes 12583040 | tf_op jit(solution)/shard_map/while/body/eval_jaxpr/scatter-add | solution.py:18
  313.3 136.3 %while.27 = (s32[]{:T(128)}, f32[16,2,128,128]{3,2,1,0:T(8,128)S(1)}, s32[256,3]{0,1:T(4,128)S(1)}, bf16[32,2,128,128]{3,2,1,0:T(8,128)(2,1)}, bf16[64,128,128]{...) while((s32[]{:T(128)}, f32[16,2,128,128]{3,2,1,0:T(8,128)S(1)}, ...), condition=%wide.region_5.7_spmd, body=%wide.region_3.6_spmd.sunk | while | flops 271059520 | bytes 26225168 | solution.py:20
  319.5 4.3 fusion.34
  323.8 6.5 %scatter_fusion.1 = f32[16,2,128,128]{3,2,1,0:T(8,128)S(1)} fusion(f32[16,2,128,128]{3,2,1,0:T(8,128)S(1)} %get-tuple-element.341, s32[32]{0:T(128)S(1)} %get-tuple-element.300, f32[32,2,128,128]{3,2,1,0:T(8,128)} %fusion.34), kind=kCustom, calls=%fused_computation.6.clone.1 | custom fusion | flops 1048576 | bytes 12583040 | tf_op jit(solution)/shard_map/while/body/eval_jaxpr/scatter-add | solution.py:18
  336.5 4.3 fusion.34
  340.8 6.5 %scatter_fusion.1 = f32[16,2,128,128]{3,2,1,0:T(8,128)S(1)} fusion(f32[16,2,128,128]{3,2,1,0:T(8,128)S(1)} %get-tuple-element.341, s32[32]{0:T(128)S(1)} %get-tuple-element.300, f32[32,2,128,128]{3,2,1,0:T(8,128)} %fusion.34), kind=kCustom, calls=%fused_computation.6.clone.1 | custom fusion | flops 1048576 | bytes 12583040 | tf_op jit(solution)/shard_map/while/body/eval_jaxpr/scatter-add | solution.py:18
  353.5 4.3 fusion.34
  357.9 6.5 %scatter_fusion.1 = f32[16,2,128,128]{3,2,1,0:T(8,128)S(1)} fusion(f32[16,2,128,128]{3,2,1,0:T(8,128)S(1)} %get-tuple-element.341, s32[32]{0:T(128)S(1)} %get-tuple-element.300, f32[32,2,128,128]{3,2,1,0:T(8,128)} %fusion.34), kind=kCustom, calls=%fused_computation.6.clone.1 | custom fusion | flops 1048576 | bytes 12583040 | tf_op jit(solution)/shard_map/while/body/eval_jaxpr/scatter-add | solution.py:18
  374.9 6.5 %scatter_fusion.1 = f32[16,2,128,128]{3,2,1,0:T(8,128)S(1)} fusion(f32[16,2,128,128]{3,2,1,0:T(8,128)S(1)} %get-tuple-element.341, s32[32]{0:T(128)S(1)} %get-tuple-element.300, f32[32,2,128,128]{3,2,1,0:T(8,128)} %fusion.34), kind=kCustom, calls=%fused_computation.6.clone.1 | custom fusion | flops 1048576 | bytes 12583040 | tf_op jit(solution)/shard_map/while/body/eval_jaxpr/scatter-add | solution.py:18
  387.6 4.3 fusion.34
  391.9 6.5 %scatter_fusion.1 = f32[16,2,128,128]{3,2,1,0:T(8,128)S(1)} fusion(f32[16,2,128,128]{3,2,1,0:T(8,128)S(1)} %get-tuple-element.341, s32[32]{0:T(128)S(1)} %get-tuple-element.300, f32[32,2,128,128]{3,2,1,0:T(8,128)} %fusion.34), kind=kCustom, calls=%fused_computation.6.clone.1 | custom fusion | flops 1048576 | bytes 12583040 | tf_op jit(solution)/shard_map/while/body/eval_jaxpr/scatter-add | solution.py:18
  409.0 6.5 %scatter_fusion.1 = f32[16,2,128,128]{3,2,1,0:T(8,128)S(1)} fusion(f32[16,2,128,128]{3,2,1,0:T(8,128)S(1)} %get-tuple-element.341, s32[32]{0:T(128)S(1)} %get-tuple-element.300, f32[32,2,128,128]{3,2,1,0:T(8,128)} %fusion.34), kind=kCustom, calls=%fused_computation.6.clone.1 | custom fusion | flops 1048576 | bytes 12583040 | tf_op jit(solution)/shard_map/while/body/eval_jaxpr/scatter-add | solution.py:18
  421.7 4.3 fusion.34
  426.0 6.5 %scatter_fusion.1 = f32[16,2,128,128]{3,2,1,0:T(8,128)S(1)} fusion(f32[16,2,128,128]{3,2,1,0:T(8,128)S(1)} %get-tuple-element.341, s32[32]{0:T(128)S(1)} %get-tuple-element.300, f32[32,2,128,128]{3,2,1,0:T(8,128)} %fusion.34), kind=kCustom, calls=%fused_computation.6.clone.1 | custom fusion | flops 1048576 | bytes 12583040 | tf_op jit(solution)/shard_map/while/body/eval_jaxpr/scatter-add | solution.py:18
  438.7 4.3 fusion.34
  443.0 6.5 %scatter_fusion.1 = f32[16,2,128,128]{3,2,1,0:T(8,128)S(1)} fusion(f32[16,2,128,128]{3,2,1,0:T(8,128)S(1)} %get-tuple-element.341, s32[32]{0:T(128)S(1)} %get-tuple-element.300, f32[32,2,128,128]{3,2,1,0:T(8,128)} %fusion.34), kind=kCustom, calls=%fused_computation.6.clone.1 | custom fusion | flops 1048576 | bytes 12583040 | tf_op jit(solution)/shard_map/while/body/eval_jaxpr/scatter-add | solution.py:18
  450.9 176.9 %all-gather.9.cloned.1.call-done = f32[128,2,128,128]{3,2,1,0:T(8,128)} async-done(((f32[16,2,128,128]{3,2,1,0:T(8,128)}), f32[128,2,128,128]{3,2,1,0:T(8,128)}) %all-gather.9.cloned.1.call-update) | async-done | bytes 16777232 | tf_op jit(solution)/shard_map/all_gather | solution.py:52
  627.8 7.9 %reduce_sum.9 = f32[16,2,128,128]{3,2,1,0:T(8,128)S(1)} reduce(f32[8,16,2,128,128]{4,3,2,1,0:T(8,128)} %bitcast.61, f32[]{:T(128)} %constant.155.clone.1), dimensions={0}, to_apply=%region_6.8 | reduce | flops 3670016 | bytes 18874372 | tf_op jit(solution)/shard_map/reduce_sum | solution.py:53
  (116 shorter events, 85.6 us)
Async XLA Ops:
  6.5 1.4 copy-start
  22.0 13.9 %copy-start.4 = (s32[1,1,96,3]{2,1,3,0:T(1,128)S(1)}, s32[1,1,96,3]{2,1,3,0:T(1,128)}, u32[]{:S(2)}) copy-start(s32[1,1,96,3]{2,1,3,0:T(1,128)} %param.16) | copy-start | bytes 3460
  22.0 13.9 %copy-start.3 = (s32[1,1,256,3]{2,1,3,0:T(1,128)S(1)}, s32[1,1,256,3]{2,1,3,0:T(1,128)}, u32[]{:S(2)}) copy-start(s32[1,1,256,3]{2,1,3,0:T(1,128)} %param.17) | copy-start | bytes 9220
  22.0 208.9 %all-to-all-start = ((bf16[128,2,128,128]{3,2,1,0:T(8,128)(2,1)}), bf16[128,2,128,128]{3,2,1,0:T(8,128)(2,1)}, u32[]{:S(2)}, u32[]{:S(2)}) async-start(bf16[128,2,128,128]{3,2,1,0:T(8,128)(2,1)} %select_select_fusion), calls=%async_computation | async-start | bytes 16777216 | tf_op jit(solution)/shard_map/all_to_all | solution.py:45
  34.1 110.9 %all-gather.5.cloned.1.call-start = ((), (), s32[]{:S(2)}) async-start(), calls=%async_computation.1 | async-start | bytes 2129920 | tf_op jit(solution)/shard_map/all_gather | solution.py:33
  34.9 278.2 %all-gather.7.cloned.1.call-start = ((), (), s32[]{:S(2)}) async-start(), calls=%async_computation.2 | async-start | bytes 2129920 | tf_op jit(solution)/shard_map/all_gather | solution.py:34
  35.6 592.2 %all-gather.9.cloned.1.call-start = ((), (), s32[]{:S(2)}) async-start(), calls=%async_computation.3 | async-start | bytes 18874368 | tf_op jit(solution)/shard_map/all_gather | solution.py:52
  449.5 1.3 copy-start.2
  627.8 8.6 %copy-start.1 = (bf16[16,2,128,128]{3,2,1,0:T(8,128)(2,1)S(1)}, bf16[16,2,128,128]{3,2,1,0:T(8,128)(2,1)}, u32[]{:S(2)}) copy-start(bf16[16,2,128,128]{3,2,1,0:T(8,128)(2,1)} %param.12) | copy-start | bytes 3145732
Sparse Core Ops, SparseCore 0:
  38.3 106.6 all-gather.4
  148.4 89.1 all-gather.6
  451.0 176.7 all-gather.8
